TPU v7x, 256 devices: a whole 4x4x8 slice. The times are simulated.
256 devices in a mesh: front: 4 (over x), row: 8 (over z_hi, core), col: 8 (over y, z_lo).
Axes of the slice: x: 4, y: 4, z: 8 (z_hi: 4, z_lo: 2; z = z_hi * 2 + z_lo), core: 2. Of those that a mesh axis runs over, the one named last changes fastest.
Arguments:
- front: bfloat16 [4, 12288, 12288], P('front', 'row', 'col'), may hold values from -6 to 6
- panel: bfloat16 [4, 12288, 512], P('front', ('row', 'col')), may hold values from -8 to 8
- inverse: bfloat16 [4, 512, 512], P('front'), may hold values from -0.0046 to 0.056
- fill: int32 [4, 48], P('front'), may hold values 0 or 1
- block_map: int32 [4, 48], P('front'), may hold values from 0 to 47, as said below
- parent_front: bfloat16 [4, 6144, 12288], P('front', 'row', 'col'), may hold values from -6 to 6
Outputs:
- factor_rows: bfloat16 [4, 12288, 512], P('front', ('row', 'col'))
- parent: float32 [4, 6144, 12288], P('front', 'row', 'col')
Inputs may be any that keep to these rules, and one draw needn't show every extreme that they name: `block_map`: each front's map is a permutation of its blocks that keeps every aligned group of 6 blocks in place as a group.
All inputs are finite; a program needn't handle non-finite values. No bound on the sum of `fill` on one device may be relied on, other than what follows from the above.
Results may differ from a plain program's by a relative error of at most 0.0025.
Values may be sent and summed in bfloat16 or wider, within the bound.
A program may use at most 64 MiB of HBM per device.

v0:
```python
import jax
import jax.numpy as jnp
from jax import lax
from jax.sharding import PartitionSpec as P

BLK = 256


def from_partner(block, axis, distance):
    count = lax.axis_size(axis)
    route = []
    for low in range(count):
        high = low | 1 << distance
        if high != low and high < count:
            route += [(low, high), (high, low)]
    return lax.ppermute(block, axis, route)


def block_inverse(mapping, block_total):
    target = jnp.arange(block_total, dtype=jnp.int32)
    matches = (mapping[:, None] == target[None, :]).astype(jnp.int32)
    return jnp.sum(matches * target[:, None], axis=0)


def shards(front, panel, inverse, fill, block_map, parent_front):
    col_count = lax.axis_size("col")
    row_index = lax.axis_index("row")
    col_index = lax.axis_index("col")
    local_rows = panel.shape[1]
    tile_rows = front.shape[1]
    tile_cols = front.shape[2]
    block_total = fill.shape[1]
    first_row = (row_index * col_count + col_index) * local_rows
    positions = (first_row + jnp.arange(local_rows, dtype=jnp.int32)) // BLK
    blocks = jnp.arange(block_total, dtype=jnp.int32)
    row_fill = jnp.sum(
        (positions[:, None] == blocks[None, :]).astype(jnp.int32) * fill[0][None, :], axis=1
    )
    masked = panel[0] * row_fill[:, None].astype(jnp.bfloat16)
    factor = jnp.dot(masked, jnp.triu(inverse[0]), preferred_element_type=jnp.float32).astype(
        jnp.bfloat16
    )
    all_rows = lax.all_gather(factor, ("row", "col"), axis=0, tiled=True)
    row_side = lax.dynamic_slice_in_dim(all_rows, row_index * tile_rows, tile_rows, 0)
    col_side = lax.dynamic_slice_in_dim(all_rows, col_index * tile_cols, tile_cols, 0)
    contract = (((1,), (1,)), ((), ()))
    initial = front[0].astype(jnp.float32)
    row_blocks = tile_rows // BLK
    col_blocks = tile_cols // BLK
    update = lax.dot_general(row_side, col_side, contract, preferred_element_type=jnp.float32)
    schur = initial - update
    source = block_inverse(block_map[0], block_total)
    row_source = (
        lax.dynamic_slice_in_dim(source, row_index * row_blocks, row_blocks, 0)
        - row_index * row_blocks
    )
    col_source = (
        lax.dynamic_slice_in_dim(source, col_index * col_blocks, col_blocks, 0)
        - col_index * col_blocks
    )
    shaped = jnp.take(schur.reshape(row_blocks, BLK, tile_cols), row_source, axis=0)
    shaped = jnp.take(shaped.reshape(tile_rows, col_blocks, BLK), col_source, axis=1)
    contribution = shaped.reshape(tile_rows, tile_cols).astype(jnp.bfloat16)
    half_rows = tile_rows // 2
    parity = lax.axis_index("front") % 2
    kept_half = lax.dynamic_slice_in_dim(contribution, parity * half_rows, half_rows, 0)
    sent_half = lax.dynamic_slice_in_dim(contribution, (1 - parity) * half_rows, half_rows, 0)
    arrived = from_partner(sent_half, "front", 0)
    parent = (
        parent_front[0].astype(jnp.float32)
        + kept_half.astype(jnp.float32)
        + arrived.astype(jnp.float32)
    )
    return (factor[None], parent[None])


def solution(mesh):
    placed = (
        P("front", "row", "col"),
        P("front", ("row", "col"), None),
        P("front", None, None),
        P("front", None),
        P("front", None),
        P("front", "row", "col"),
    )
    return jax.shard_map(
        shards,
        mesh=mesh,
        in_specs=placed,
        out_specs=(P("front", ("row", "col"), None), P("front", "row", "col")),
        check_vma=False,
    )
```

profile of v0, /device:TPU:105, one launch (start us, length us, event | category | flops | bytes accessed | tf_op | source)
XLA Modules:
  0.0 335.8 jit_solution(6356897594682309380)
XLA Ops:
  7.2 0.0 all-gather.2.cloned.1.call-start
  7.2 0.7 select_reduce_fusion
  8.0 2.2 convolution_convert_fusion
  10.2 0.0 all-gather.2.cloned.1.call-update
  10.2 0.7 select_reduce_fusion.1
  11.0 0.1 compare_and_fusion.1
  11.1 0.1 broadcast_in_dim.52
  11.1 0.1 broadcast_in_dim.49
  11.3 204.7 %all-gather.2.cloned.1.call-done = bf16[12288,512]{1,0:T(8,128)(2,1)} async-done(((bf16[192,512]{1,0:T(8,128)(2,1)}), bf16[12288,512]{1,0:T(8,128)(2,1)}) %all-gather.2.cloned.1.call-update) | async-done | bytes 12582928 | tf_op jit(solution)/shard_map/all_gather | solution.py:43
  216.0 8.2 %convert_subtract_fusion = bf16[1536,1536]{1,0:T(8,128)(2,1)} fusion(bf16[1,1536,1536]{2,1,0:T(8,128)(2,1)} %param.6, bf16[12288,512]{1,0:T(8,128)(2,1)} %all-gather.2.cloned.1.call-done, s32[]{:T(128)S(6)} %select_n.68, s32[]{:T(128)S(6)} %select_n.67), kind=kOutput, calls=%fused_computation.2 | convolution fusion | flops 2422996992 | bytes 12582920 | tf_op jit(solution)/shard_map/dot_general | solution.py:50
  224.1 5.5 %gather_fusion = bf16[6,256,1536]{2,1,0:T(8,128)(2,1)} fusion(bf16[6,256,1536]{2,1,0:T(8,128)(2,1)} %bitcast.24, s32[1024]{0:T(1024)S(1)} %pad_clamp_fusion.1), kind=kCustom, calls=%fused_computation | custom fusion | bytes 9437208 | tf_op jit(solution)/shard_map/jit(_take)/gather | solution.py:61
  229.7 10.3 %gather.13 = bf16[1536,6,256]{2,1,0:T(8,128)(2,1)} reshape(bf16[6,256,1536]{2,1,0:T(8,128)(2,1)} %gather_fusion) | data formatting | bytes 9437184 | tf_op jit(solution)/shard_map/jit(_take)/gather | solution.py:61
  240.0 5.9 %copy_select_fusion = bf16[1536,6,256]{2,0,1:T(8,128)(2,1)} fusion(bf16[1536,6,256]{2,1,0:T(8,128)(2,1)} %gather.13, pred[1536]{0:T(1024)(128)(4,1)S(1)} %broadcast_in_dim.53), kind=kLoop, calls=%fused_computation.5 | loop fusion | flops 2359296 | bytes 9438720 | tf_op jit(solution)/shard_map/jit(_take)/select_n | solution.py:61
  245.8 5.5 %gather_fusion.1 = bf16[6,1536,256]{2,1,0:T(8,128)(2,1)} fusion(bf16[1536,6,256]{2,0,1:T(8,128)(2,1)} %copy_select_fusion, s32[1024]{0:T(1024)S(1)} %pad_clamp_fusion), kind=kCustom, calls=%fused_computation.1 | custom fusion | bytes 9437208 | tf_op jit(solution)/shard_map/jit(_take)/gather | solution.py:62
  251.3 6.6 %copy.14 = bf16[1536,6,256]{0,2,1:T(8,128)(2,1)} copy(bf16[1536,6,256]{2,0,1:T(8,128)(2,1)} %bitcast.23) | data formatting | bytes 9437184 | tf_op jit(solution)/shard_map/jit(_take)/gather | solution.py:62
  257.9 3.2 fusion
  261.1 0.0 copy-start
  261.1 2.2 copy-done
  263.3 1.6 constant_dynamic-slice_fusion
  264.8 1.2 collective-permute-start
  266.0 2.8 copy.12
  268.9 48.8 %collective-permute-done = bf16[768,1536]{0,1:T(8,128)(2,1)} collective-permute-done((bf16[768,1536]{0,1:T(8,128)(2,1)}, bf16[768,1536]{0,1:T(8,128)(2,1)}, u32[]{:S(2)}, u32[]{:S(2)}) %collective-permute-start) | collective-permute-done | bytes 2359328 | tf_op jit(solution)/shard_map/ppermute | solution.py:16
  317.6 5.3 %fusion.2 = f32[1,768,1536]{1,2,0:T(8,128)} fusion(bf16[768,1536]{0,1:T(8,128)(2,1)} %collective-permute-done, bf16[1,768,1536]{1,2,0:T(8,128)(2,1)S(1)} %copy.12, bf16[1536,1536]{0,1:T(8,128)(2,1)} %copy-done, s32[]{:T(128)S(6)} %select_n.72), kind=kLoop, calls=%fused_computation.8 | loop fusion | flops 5898240 | bytes 11796484 | tf_op jit(solution)/shard_map/broadcast_in_dim | solution.py:74
  322.9 6.0 %copy.15 = f32[1,768,1536]{2,1,0:T(8,128)} copy(f32[1,768,1536]{1,2,0:T(8,128)} %fusion.2) | data formatting | bytes 9437184
  (7 shorter events, 0.1 us)
Async XLA Ops:
  7.2 208.8 %all-gather.2.cloned.1.call-start = ((), (), s32[]{:S(2)}) async-start(), calls=%async_computation | async-start | bytes 12779520 | tf_op jit(solution)/shard_map/all_gather | solution.py:43
  261.1 2.2 copy-start
  264.8 52.8 %collective-permute-start = (bf16[768,1536]{0,1:T(8,128)(2,1)}, bf16[768,1536]{0,1:T(8,128)(2,1)}, u32[]{:S(2)}, u32[]{:S(2)}) collective-permute-start(bf16[768,1536]{0,1:T(8,128)(2,1)} %constant_dynamic-slice_fusion), channel_id=1, source_target_pairs={{0,64},{64,0},{128,192},{192,128},{1,65},{65,1},{129,193},{193,129... | collective-permute-start | bytes 7077896 | tf_op jit(solution)/shard_map/ppermute | solution.py:16
Sparse Core Ops, SparseCore 0:
  10.4 205.5 all-gather.1
where the time goes:
time: 337 us; the launch traced here: 336 us
  waiting for transfers between devices  253 us (75%)
  local copies, waits for them, and re-layouts  40.7 us (12%)
  other arithmetic  15.9 us (5%)
  between operations  14.1 us (4%)
  matrix products  10.4 us (3%)
    all_gather x1, waiting for transfers between devices, shards(): all_rows = lax.all_gather(factor, ('row', 'col'), axis=0, tiled=True)  205 us
    ppermute x1, waiting for transfers between devices, from_partner(): return lax.ppermute(block, axis, route)  48.8 us
    gather x2, local copies, waits for them, and re-layouts, shards(): jnp.take(schur.reshape(row_blocks, BLK, tile_cols), row_source, axis=0)  15.8 us
    gather x2, local copies, waits for them, and re-layouts, shards(): jnp.take(shaped.reshape(tile_rows, col_blocks, BLK), col_source, axis=1)  12.1 us
    unnamed x4, local copies, waits for them, and re-layouts  11.1 us
    dot_general x1, matrix products, shards(): lax.dot_general(row_side, col_side, contract, preferred_element_type=jnp....  8.18 us
  transfers between devices with their start and end apart: 2, of which 2 were waited for; matrix products, arithmetic and copies ran while one was open for 1% of the time, Pallas kernels for 0%

commit v1 on v0

--- a/solution.py
+++ b/solution.py
@@ -4,6 +4,11 @@
 from jax.sharding import PartitionSpec as P
 
 BLK = 256
+
+
+def all_by_exchange(x, axis, along):
+    sent = jnp.stack([x] * lax.axis_size(axis))
+    return jnp.concatenate(lax.all_to_all(sent, axis, 0, 0), axis=along)
 
 
 def from_partner(block, axis, distance):
@@ -40,7 +45,7 @@
     factor = jnp.dot(masked, jnp.triu(inverse[0]), preferred_element_type=jnp.float32).astype(
         jnp.bfloat16
     )
-    all_rows = lax.all_gather(factor, ("row", "col"), axis=0, tiled=True)
+    all_rows = all_by_exchange(factor, ("row", "col"), 0)
     row_side = lax.dynamic_slice_in_dim(all_rows, row_index * tile_rows, tile_rows, 0)
     col_side = lax.dynamic_slice_in_dim(all_rows, col_index * tile_cols, tile_cols, 0)
     contract = (((1,), (1,)), ((), ()))

time: 337 us -> 413 us (1.23); the launches traced: 336 us -> 407 us
  waiting for transfers between devices: 253 us -> 322 us
  between operations: 14.1 us -> 0.76 us
  starting transfers between devices: 1.22 us -> 12.6 us
  local copies, waits for them, and re-layouts: 40.7 us -> 46.7 us
    all_to_all x0 -> x1, waiting for transfers between devices: none -> 273 us  [all_by_exchange(): return jnp.concatenate(lax.all_to_all(sent, axis, 0, 0), axis=along)]
    all_gather x1 -> x0, waiting for transfers between devices: 205 us -> none  [shards(): all_rows = lax.all_gather(factor, ('row', 'col'), axis=0, tiled=True)]
    all_to_all x0 -> x1, starting transfers between devices: none -> 11.4 us  [all_by_exchange(): return jnp.concatenate(lax.all_to_all(sent, axis, 0, 0), axis=along)]
    another operation x0 -> x1, local copies, waits for them, and re-layouts: none -> 5.99 us  [all_by_exchange(): sent = jnp.stack([x] * lax.axis_size(axis))]
    unnamed x4 -> x8, local copies, waits for them, and re-layouts: 11.1 us -> 11.1 us
where the time goes in v1:
time: 413 us; the launch traced here: 407 us
  waiting for transfers between devices  322 us (78%)
  local copies, waits for them, and re-layouts  46.7 us (11%)
  other arithmetic  15.2 us (4%)
  starting transfers between devices  12.6 us (3%)
  matrix products  9.63 us (2%)
    all_to_all x1, waiting for transfers between devices, all_by_exchange(): return jnp.concatenate(lax.all_to_all(sent, axis, 0, 0), axis=along)  273 us
    ppermute x1, waiting for transfers between devices, from_partner(): return lax.ppermute(block, axis, route)  48.3 us
    gather x2, local copies, waits for them, and re-layouts, shards(): jnp.take(schur.reshape(row_blocks, BLK, tile_cols), row_source, axis=0)  15.8 us
    gather x2, local copies, waits for them, and re-layouts, shards(): jnp.take(shaped.reshape(tile_rows, col_blocks, BLK), col_source, axis=1)  12.1 us
    all_to_all x1, starting transfers between devices, all_by_exchange(): return jnp.concatenate(lax.all_to_all(sent, axis, 0, 0), axis=along)  11.4 us
    unnamed x8, local copies, waits for them, and re-layouts  11.1 us
  transfers between devices with their start and end apart: 2, of which 2 were waited for; matrix products, arithmetic and copies ran while one was open for 1% of the time, Pallas kernels for 0%

profile of v1, /device:TPU:105, one launch (start us, length us, event | category | flops | bytes accessed | tf_op | source)
XLA Modules:
  0.0 406.6 jit_solution(563323751498706850)
XLA Ops:
  0.7 0.7 select_reduce_fusion
  1.4 1.5 convolution_convert_fusion
  2.9 0.0 copy-start.1
  2.9 6.0 %stack.2 = bf16[64,192,512]{2,1,0:T(8,128)(2,1)} broadcast(bf16[192,512]{1,0:T(8,128)(2,1)S(1)} %convolution_convert_fusion), dimensions={1,2} | broadcast | bytes 12779520 | tf_op jit(solution)/shard_map/stack | solution.py:10
  8.9 0.0 copy-done.1
  8.9 0.0 copy-start.2
  8.9 11.4 %all-to-all-start = ((bf16[64,192,512]{2,1,0:T(8,128)(2,1)}), bf16[64,192,512]{2,1,0:T(8,128)(2,1)}, u32[]{:S(2)}, u32[]{:S(2)}) async-start(bf16[64,192,512]{2,1,0:T(8,128)(2,1)} %stack.2), calls=%async_computation | async-start | bytes 25165824 | tf_op jit(solution)/shard_map/all_to_all | solution.py:11
  20.3 0.0 copy-done.2
  20.4 0.1 select_reduce_fusion.1
  20.4 0.1 compare_and_fusion.1
  20.5 0.1 broadcast_in_dim.52
  20.6 0.1 broadcast_in_dim.49
  20.7 273.4 %all-to-all-done = bf16[64,192,512]{2,1,0:T(8,128)(2,1)} async-done(((bf16[64,192,512]{2,1,0:T(8,128)(2,1)}), bf16[64,192,512]{2,1,0:T(8,128)(2,1)}, u32[]{:S(2)}, u32[]{:S(2)}) %all-to-all-start) | async-done | bytes 12582944 | tf_op jit(solution)/shard_map/all_to_all | solution.py:11
  294.1 8.1 %convert_subtract_fusion = bf16[1536,1536]{1,0:T(8,128)(2,1)} fusion(bf16[1,1536,1536]{2,1,0:T(8,128)(2,1)} %param.6, bf16[12288,512]{1,0:T(8,128)(2,1)} %bitcast.7, s32[]{:T(128)S(6)} %select_n.68, s32[]{:T(128)S(6)} %select_n.67), kind=kOutput, calls=%fused_computation.2 | convolution fusion | flops 2422996992 | bytes 12582920 | tf_op jit(solution)/shard_map/dot_general | solution.py:55
  302.2 5.6 %gather_fusion = bf16[6,256,1536]{2,1,0:T(8,128)(2,1)} fusion(bf16[6,256,1536]{2,1,0:T(8,128)(2,1)} %bitcast.25, s32[1024]{0:T(1024)S(1)} %get-tuple-element.13), kind=kCustom, calls=%fused_computation | custom fusion | bytes 9437208 | tf_op jit(solution)/shard_map/jit(_take)/gather | solution.py:66
  307.8 10.3 %gather.13 = bf16[1536,6,256]{2,1,0:T(8,128)(2,1)} reshape(bf16[6,256,1536]{2,1,0:T(8,128)(2,1)} %gather_fusion) | data formatting | bytes 9437184 | tf_op jit(solution)/shard_map/jit(_take)/gather | solution.py:66
  318.1 5.9 %copy_select_fusion = bf16[1536,6,256]{2,0,1:T(8,128)(2,1)} fusion(bf16[1536,6,256]{2,1,0:T(8,128)(2,1)} %gather.13, pred[1536]{0:T(1024)(128)(4,1)S(1)} %broadcast_in_dim.53), kind=kLoop, calls=%fused_computation.5 | loop fusion | flops 2359296 | bytes 9438720 | tf_op jit(solution)/shard_map/jit(_take)/select_n | solution.py:66
  323.9 5.5 %gather_fusion.1 = bf16[6,1536,256]{2,1,0:T(8,128)(2,1)} fusion(bf16[1536,6,256]{2,0,1:T(8,128)(2,1)} %copy_select_fusion, s32[1024]{0:T(1024)S(1)} %get-tuple-element.12), kind=kCustom, calls=%fused_computation.1 | custom fusion | bytes 9437208 | tf_op jit(solution)/shard_map/jit(_take)/gather | solution.py:67
  329.4 6.6 %copy.14 = bf16[1536,6,256]{0,2,1:T(8,128)(2,1)} copy(bf16[1536,6,256]{2,0,1:T(8,128)(2,1)} %bitcast.24) | data formatting | bytes 9437184 | tf_op jit(solution)/shard_map/jit(_take)/gather | solution.py:67
  336.0 3.2 fusion
  339.2 0.0 copy-start
  339.2 2.2 copy-done
  341.4 1.6 constant_dynamic-slice_fusion
  342.9 1.2 collective-permute-start
  344.1 2.8 copy.12
  347.0 48.3 %collective-permute-done = bf16[768,1536]{0,1:T(8,128)(2,1)} collective-permute-done((bf16[768,1536]{0,1:T(8,128)(2,1)}, bf16[768,1536]{0,1:T(8,128)(2,1)}, u32[]{:S(2)}, u32[]{:S(2)}) %collective-permute-start) | collective-permute-done | bytes 2359328 | tf_op jit(solution)/shard_map/ppermute | solution.py:21
  395.3 5.3 %fusion.2 = f32[1,768,1536]{1,2,0:T(8,128)} fusion(bf16[768,1536]{0,1:T(8,128)(2,1)} %collective-permute-done, bf16[1,768,1536]{1,2,0:T(8,128)(2,1)S(1)} %copy.12, bf16[1536,1536]{0,1:T(8,128)(2,1)} %copy-done, s32[]{:T(128)S(6)} %select_n.72), kind=kLoop, calls=%fused_computation.8 | loop fusion | flops 5898240 | bytes 11796484 | tf_op jit(solution)/shard_map/broadcast_in_dim | solution.py:79
  400.6 6.0 %copy.15 = f32[1,768,1536]{2,1,0:T(8,128)} copy(f32[1,768,1536]{1,2,0:T(8,128)} %fusion.2) | data formatting | bytes 9437184
  (6 shorter events, 0.1 us)
Async XLA Ops:
  2.9 6.0 %copy-start.1 = (bf16[192,512]{1,0:T(8,128)(2,1)}, bf16[192,512]{1,0:T(8,128)(2,1)S(1)}, u32[]{:S(2)}) copy-start(bf16[192,512]{1,0:T(8,128)(2,1)S(1)} %convolution_convert_fusion) | copy-start | bytes 589828
  8.9 11.4 %copy-start.2 = (s32[1,48]{1,0:T(1,128)S(1)}, s32[1,48]{1,0:T(1,128)}, u32[]{:S(2)}) copy-start(s32[1,48]{1,0:T(1,128)} %param.10) | copy-start | bytes 580
  8.9 285.2 %all-to-all-start = ((bf16[64,192,512]{2,1,0:T(8,128)(2,1)}), bf16[64,192,512]{2,1,0:T(8,128)(2,1)}, u32[]{:S(2)}, u32[]{:S(2)}) async-start(bf16[64,192,512]{2,1,0:T(8,128)(2,1)} %stack.2), calls=%async_computation | async-start | bytes 25165824 | tf_op jit(solution)/shard_map/all_to_all | solution.py:11
  339.2 2.2 copy-start
  342.9 52.4 %collective-permute-start = (bf16[768,1536]{0,1:T(8,128)(2,1)}, bf16[768,1536]{0,1:T(8,128)(2,1)}, u32[]{:S(2)}, u32[]{:S(2)}) collective-permute-start(bf16[768,1536]{0,1:T(8,128)(2,1)} %constant_dynamic-slice_fusion), channel_id=1, source_target_pairs={{0,64},{64,0},{128,192},{192,128},{1,65},{65,1},{129,193},{193,129... | collective-permute-start | bytes 7077896 | tf_op jit(solution)/shard_map/ppermute | solution.py:21
